TPU v7x, 256 devices: a whole 4x4x8 slice. The times are simulated.
256 devices in a mesh: lat: 16 (over y_lo, x, core), lon: 16 (over z, y_hi).
Axes of the slice: x: 4, y: 4 (y_hi: 2, y_lo: 2; y = y_hi * 2 + y_lo), z: 8, core: 2. Of those that a mesh axis runs over, the one named last changes fastest.
Arguments:
- fields: bfloat16 [512, 512, 256], P('lat', 'lon'), may hold values from -6 to 6
- w_conv1: bfloat16 [3, 3, 256, 256], replicated, may hold values from -0.125 to 0.125
- b_conv1: float32 [256], replicated, may hold values from -3 to 3
- w_conv2: bfloat16 [3, 3, 256, 256], replicated, may hold values from -0.125 to 0.125
- b_conv2: float32 [256], replicated, may hold values from -3 to 3
- w_query: bfloat16 [256, 256], replicated, may hold values from -16 to 16
- w_key: bfloat16 [256, 64], replicated, may hold values from -1 to 1
- w_value: bfloat16 [256, 64], replicated, may hold values from -0.375 to 0.375
- w_out: bfloat16 [256, 256], replicated, may hold values from -0.375 to 0.375
- rotation: int32 [16, 16], replicated, may hold values from 0 to 3
- owner: int32 [16, 16], replicated, may hold values from 0 to 15, as said below
- counts: int32 [512], replicated, may hold values from 4 to 512
Outputs:
- fields_out: bfloat16 [512, 512, 256], P('lat', 'lon')
Inputs may be any that keep to these rules, and one draw needn't show every extreme that they name: Each row of owner holds every number from 0 to 15 exactly once.
All inputs are finite; a program needn't handle non-finite values.
Results may differ from a plain program's by a relative error of at most 0.014.
Values may be sent and summed in bfloat16 or wider, within the bound.
A program may use at most 64 MiB of HBM per device.

v0:
```python
import math
import jax
import jax.numpy as jnp
from jax import lax
from jax.sharding import PartitionSpec as P


def shortened(x):

    def short(part):
        return part.astype(jnp.bfloat16) if part.dtype == jnp.float32 else part

    return jax.tree.map(short, x)


def passed_along(x, axis, by):
    devices = lax.axis_size(axis)
    pairs = [(i, i + by) for i in range(devices) if 0 <= i + by < devices]
    return lax.ppermute(x, axis, pairs)


def turn_block(block, quarter_turns):
    options = [lambda m, k=k: jnp.rot90(m, k, axes=(0, 1)) for k in range(4)]
    return lax.switch(quarter_turns % 4, options, block)


def inverse_owner(owner):
    shards = jnp.arange(owner.shape[1], dtype=jnp.int32)
    matches = owner[:, None, :] == shards[None, :, None]
    return jnp.sum(jnp.where(matches, shards[None, None, :], 0), axis=2)


def live_region(counts, first_row, row_count, first_col, col_count, total_cols):
    padded_counts = jnp.pad(counts, 2)
    row_limits = lax.dynamic_slice_in_dim(padded_counts, first_row + 2, row_count)
    columns = (first_col + jnp.arange(col_count, dtype=jnp.int32)) % total_cols
    return (columns[None, :] < row_limits[:, None]).astype(jnp.float32)


def pick_block(stack, inverse, band_row, segment):
    return lax.dynamic_index_in_dim(stack, inverse[band_row, segment], 0, keepdims=False)


def fetch_halo(part, width, inverse, band_index, segment):
    lat_size = lax.axis_size("lat")
    lon_size = lax.axis_size("lon")
    block_size = part.shape[0]
    chans = part.shape[2]
    from_north = passed_along(shortened(part[-width:]), "lat", 1)
    from_south = passed_along(shortened(part[:width]), "lat", -1)
    west_all, east_all, north_all, south_all = (
        lax.all_gather(shortened(part[:, :width]), "lon", axis=0, tiled=True),
        lax.all_gather(shortened(part[:, -width:]), "lon", axis=0, tiled=True),
        lax.all_gather(shortened(from_north), "lon", axis=0, tiled=True).astype(from_north.dtype),
        lax.all_gather(shortened(from_south), "lon", axis=0, tiled=True).astype(from_south.dtype),
    )
    west_all = west_all.reshape(lon_size, block_size, width, chans)
    east_all = east_all.reshape(lon_size, block_size, width, chans)
    north_all = north_all.reshape(lon_size, width, block_size, chans)
    south_all = south_all.reshape(lon_size, width, block_size, chans)
    west_segment = (segment - 1) % lon_size
    east_segment = (segment + 1) % lon_size
    north_band = jnp.maximum(band_index - 1, 0)
    south_band = jnp.minimum(band_index + 1, lat_size - 1)
    left_cols = pick_block(east_all, inverse, band_index, west_segment)
    right_cols = pick_block(west_all, inverse, band_index, east_segment)
    upper = jnp.concatenate(
        [
            pick_block(north_all, inverse, north_band, west_segment)[:, -width:],
            pick_block(north_all, inverse, north_band, segment),
            pick_block(north_all, inverse, north_band, east_segment)[:, :width],
        ],
        axis=1,
    )
    lower = jnp.concatenate(
        [
            pick_block(south_all, inverse, south_band, west_segment)[:, -width:],
            pick_block(south_all, inverse, south_band, segment),
            pick_block(south_all, inverse, south_band, east_segment)[:, :width],
        ],
        axis=1,
    )
    middle = jnp.concatenate([left_cols, part, right_cols], axis=1)
    return jnp.concatenate([upper, middle, lower], axis=0)


def convolve(padded, weight, bias, out_rows, out_cols):
    chans = padded.shape[2]
    total = jnp.zeros((out_rows * out_cols, chans), jnp.float32) + bias
    for i in range(3):
        for j in range(3):
            window = padded[i : i + out_rows, j : j + out_cols].reshape(out_rows * out_cols, chans)
            total = total + jnp.dot(window, weight[i, j], preferred_element_type=jnp.float32)
    return total.reshape(out_rows, out_cols, chans)


def on_device(
    fields,
    w_conv1,
    b_conv1,
    w_conv2,
    b_conv2,
    w_query,
    w_key,
    w_value,
    w_out,
    rotation,
    owner,
    counts,
):
    block_size = fields.shape[0]
    chans = fields.shape[2]
    head_dim = w_key.shape[1]
    heads = chans // head_dim
    lon_size = lax.axis_size("lon")
    band_index = lax.axis_index("lat")
    shard_index = lax.axis_index("lon")
    quarter = rotation[band_index, shard_index]
    segment = owner[band_index, shard_index]
    owner_row = owner[band_index]
    inverse = inverse_owner(owner)
    upright = turn_block(fields, (4 - quarter) % 4)
    total_cols = block_size * lon_size
    first_row = band_index * block_size
    first_col = segment * block_size
    live_own = live_region(counts, first_row, block_size, first_col, block_size, total_cols)[
        :, :, None
    ]
    padded = fetch_halo(upright, 1, inverse, band_index, segment)
    first = convolve(padded, w_conv1, b_conv1, block_size, block_size)
    act = (jax.nn.silu(first) * live_own).astype(jnp.bfloat16)
    act_padded = fetch_halo(act, 1, inverse, band_index, segment)
    second = convolve(act_padded, w_conv2, b_conv2, block_size, block_size)
    mixed = ((upright.astype(jnp.float32) + second) * live_own).astype(jnp.bfloat16)
    flat = mixed.reshape(block_size * block_size, chans).astype(jnp.float32)
    normed = (flat * lax.rsqrt(jnp.mean(flat * flat, axis=1, keepdims=True) + 1e-06)).astype(
        jnp.bfloat16
    )
    query = jnp.dot(normed, w_query, preferred_element_type=jnp.float32).astype(jnp.bfloat16)
    query = query.reshape(block_size, block_size, chans)
    key_val = jnp.dot(
        normed, jnp.concatenate([w_key, w_value], axis=1), preferred_element_type=jnp.float32
    )
    key_val = key_val.astype(jnp.bfloat16).reshape(block_size, block_size, 2 * head_dim)
    root_dim = math.sqrt(head_dim)
    heads_q = query.reshape(block_size, block_size, heads, head_dim)
    row_limits = lax.dynamic_slice_in_dim(counts, first_row, block_size)
    piece = lax.all_gather(key_val, "lon", axis=1, tiled=True)
    summed = jnp.zeros((block_size, block_size, heads, head_dim), jnp.float32)
    peak = jnp.full((block_size, block_size, heads), -jnp.inf, jnp.float32)
    total = jnp.zeros((block_size, block_size, heads), jnp.float32)
    positions = jnp.arange(piece.shape[1], dtype=jnp.int32)
    true_cols = owner_row[positions // block_size] * block_size + positions % block_size
    live_keys = true_cols[None, :] < row_limits[:, None]
    scores = (
        jnp.einsum(
            "rchd,rkd->rchk", heads_q, piece[:, :, :head_dim], preferred_element_type=jnp.float32
        )
        / root_dim
    )
    scores = jnp.where(live_keys[:, None, None, :], scores, -jnp.inf)
    new_peak = jnp.max(scores, axis=3)
    safe_peak = jnp.where(jnp.isfinite(new_peak), new_peak, 0.0)
    expo = jnp.exp(scores - safe_peak[..., None])
    shrink = jnp.exp(peak - safe_peak)
    total = total * shrink + jnp.sum(expo, axis=3)
    summed = summed * shrink[..., None] + jnp.einsum(
        "rchk,rkd->rchd",
        expo.astype(jnp.bfloat16),
        piece[:, :, head_dim:],
        preferred_element_type=jnp.float32,
    )
    summed, peak, total = (summed, new_peak, total)
    attended = (
        (summed / total[..., None]).astype(jnp.bfloat16).reshape(block_size * block_size, chans)
    )
    update = jnp.dot(attended, w_out, preferred_element_type=jnp.float32).reshape(
        block_size, block_size, chans
    )
    result = (mixed.astype(jnp.float32) + update * live_own).astype(jnp.bfloat16)
    return turn_block(result, quarter)


def solution(mesh):
    in_specs = (P("lat", "lon", None), P(), P(), P(), P(), P(), P(), P(), P(), P(), P(), P())
    out_specs = P("lat", "lon", None)
    return jax.shard_map(
        on_device, mesh=mesh, in_specs=in_specs, out_specs=out_specs, check_vma=False
    )
```

profile of v0, /device:TPU:2, one launch (start us, length us, event | category | flops | bytes accessed | tf_op | source)
XLA Modules:
  0.0 503.1 jit_solution(5571521871443634493)
XLA Ops:
  6.5 1.3 dynamic_slice.73
  8.5 1.1 conditional.2
  8.6 1.1 rev.22
  10.0 1.9 collective-permute-start.1
  11.9 2.4 collective-permute-start
  14.3 0.6 dynamic_slice.74
  18.2 0.3 select_reduce_fusion
  19.2 0.7 fusion.83
  22.9 46.0 %all_gather.28 = bf16[512,1,256]{2,0,1:T(8,128)(2,1)S(1)} all-gather(bf16[32,1,256]{2,0,1:T(8,128)(2,1)S(1)} %get-tuple-element.55), channel_id=1, replica_groups=mesh['lat'=16,'lon'=16] {'lon'}, dimensions={0}, use_global_device_ids=true | all-gather | bytes 278528 | tf_op jit(solution)/shard_map/all_gather | solution.py:53
  69.6 36.9 %all_gather.29 = bf16[512,1,256]{2,0,1:T(8,128)(2,1)S(1)} all-gather(bf16[32,1,256]{2,0,1:T(8,128)(2,1)S(1)} %get-tuple-element.56), channel_id=1, replica_groups=mesh['lat'=16,'lon'=16] {'lon'}, dimensions={0}, use_global_device_ids=true | all-gather | bytes 278528 | tf_op jit(solution)/shard_map/all_gather | solution.py:52
  107.3 0.4 pad_maximum_fusion.2
  119.1 40.5 %all_gather.27 = bf16[16,32,256]{2,1,0:T(8,128)(2,1)S(1)} all-gather(bf16[1,32,256]{2,1,0:T(8,128)(2,1)S(1)} %collective-permute-done), channel_id=1, replica_groups=mesh['lat'=16,'lon'=16] {'lon'}, dimensions={0}, use_global_device_ids=true | all-gather | bytes 278528 | tf_op jit(solution)/shard_map/all_gather | solution.py:54
  159.7 37.0 %all_gather.30 = bf16[16,32,256]{2,1,0:T(8,128)(2,1)S(1)} all-gather(bf16[1,32,256]{2,1,0:T(8,128)(2,1)S(1)} %collective-permute-done.1), channel_id=1, replica_groups=mesh['lat'=16,'lon'=16] {'lon'}, dimensions={0}, use_global_device_ids=true | all-gather | bytes 278528 | tf_op jit(solution)/shard_map/all_gather | solution.py:55
  196.7 0.5 maximum_maximum_fusion.1
  197.2 0.8 fusion.77
  198.0 0.4 copy-done.4
  201.5 1.9 collective-permute-start.3
  203.5 2.4 collective-permute-start.2
  205.9 40.5 %all_gather.33 = bf16[512,1,256]{2,0,1:T(8,128)(2,1)S(1)} all-gather(bf16[32,1,256]{2,0,1:T(8,128)(2,1)S(1)} %copy.114), channel_id=1, replica_groups=mesh['lat'=16,'lon'=16] {'lon'}, dimensions={0}, use_global_device_ids=true | all-gather | bytes 278528 | tf_op jit(solution)/shard_map/all_gather | solution.py:52
  246.4 37.2 %all_gather.32 = bf16[512,1,256]{2,0,1:T(8,128)(2,1)S(1)} all-gather(bf16[32,1,256]{2,0,1:T(8,128)(2,1)S(1)} %copy.113), channel_id=1, replica_groups=mesh['lat'=16,'lon'=16] {'lon'}, dimensions={0}, use_global_device_ids=true | all-gather | bytes 278528 | tf_op jit(solution)/shard_map/all_gather | solution.py:53
  283.7 0.4 pad_maximum_fusion
  284.2 40.2 %all_gather.31 = bf16[16,32,256]{2,1,0:T(8,128)(2,1)S(1)} all-gather(bf16[1,32,256]{2,1,0:T(8,128)(2,1)S(1)} %collective-permute-done.2), channel_id=1, replica_groups=mesh['lat'=16,'lon'=16] {'lon'}, dimensions={0}, use_global_device_ids=true | all-gather | bytes 278528 | tf_op jit(solution)/shard_map/all_gather | solution.py:54
  324.4 37.5 %all_gather.34 = bf16[16,32,256]{2,1,0:T(8,128)(2,1)S(1)} all-gather(bf16[1,32,256]{2,1,0:T(8,128)(2,1)S(1)} %collective-permute-done.3), channel_id=1, replica_groups=mesh['lat'=16,'lon'=16] {'lon'}, dimensions={0}, use_global_device_ids=true | all-gather | bytes 278528 | tf_op jit(solution)/shard_map/all_gather | solution.py:55
  362.0 0.5 maximum_maximum_fusion.3
  362.5 0.4 fusion.75
  362.9 0.4 fusion.76
  363.3 0.9 copy-done.5
  365.3 0.5 convolution_add_fusion.4
  367.0 0.5 multiply_reduce_fusion
  367.9 0.4 copy-done.7
  368.6 0.8 copy.119
  371.5 0.7 fusion.85
  372.2 4.4 compare_select_fusion.1
  376.6 5.6 %fusion.63 = s32[512]{0:T(512)S(1)} fusion(pred[512]{0:T(512)(128)(4,1)S(1)} %get-tuple-element.95, pred[512]{0:T(512)(128)(4,1)S(1)} %get-tuple-element.96, pred[512]{0:T(512)(128)(4,1)S(1)} %get-tuple-element.97, pred[512]{0:T(512)(128)(4,1)S(1)} %get-tuple-element.98, pred[512]{0:T(512)(128)(4,1)S(1)} %get-tuple-element.99, ...), kind=kLoop, calls=%fused_computation.145 | loop fusion | flops 8704 | bytes 8740 | tf_op jit(solution)/shard_map/add | solution.py:153
  382.6 1.5 reshape_reshape.3
  384.1 82.8 %all-gather.2.cloned.1.call-done = bf16[32,512,128]{2,0,1:T(8,128)(2,1)} async-done(((bf16[32,32,128]{2,0,1:T(8,128)(2,1)}), bf16[32,512,128]{2,0,1:T(8,128)(2,1)}) %all-gather.2.cloned.1.call-update) | async-done | bytes 4194320 | tf_op jit(solution)/shard_map/all_gather | solution.py:148
  466.9 7.6 %fusion.74 = (bf16[32,512,64]{2,0,1:T(8,128)(2,1)}, bf16[32,512,64]{2,0,1:T(8,128)(2,1)}) fusion(bf16[32,512,128]{2,0,1:T(8,128)(2,1)} %all-gather.2.cloned.1.call-done), kind=kLoop, calls=%fused_computation.158 | loop fusion | bytes 8388608 | tf_op jit(solution)/shard_map/slice | solution.py:157
  474.5 4.5 copy.133
  478.9 5.5 %copy.134 = bf16[32,512,64]{1,2,0:T(8,128)(2,1)} copy(bf16[32,512,64]{2,0,1:T(8,128)(2,1)} %get-tuple-element.28) | data formatting | bytes 4194304
  484.4 2.6 fusion
  487.0 2.4 fusion.1
  489.5 2.9 divide_convert_fusion
  492.4 0.5 copy.123
  492.9 0.7 dot_general.93
  493.9 0.7 conditional.3
  493.9 0.4 rev.23
  494.6 0.8 copy-done.2
  495.4 0.9 copy-done.1
  (91 shorter events, 8.1 us)
Async XLA Ops:
  6.5 375.8 %copy-start = (bf16[256,256]{1,0:T(8,128)(2,1)S(1)}, bf16[256,256]{1,0:T(8,128)(2,1)}, u32[]{:S(2)}) copy-start(bf16[256,256]{1,0:T(8,128)(2,1)} %param.25) | copy-start | bytes 393220
  6.5 460.3 %all-gather.2.cloned.1.call-start = ((), (), s32[]{:S(2)}) async-start(), calls=%async_computation | async-start | bytes 4456448 | tf_op jit(solution)/shard_map/all_gather | solution.py:148
  8.5 5.8 %copy-start.9 = (s32[16,16]{1,0:T(8,128)S(1)}, s32[16,16]{1,0:T(8,128)}, u32[]{:S(2)}) copy-start(s32[16,16]{1,0:T(8,128)} %param.30) | copy-start | bytes 3076
  8.5 14.0 %copy-start.10 = (s32[512]{0:T(512)S(1)}, s32[512]{0:T(512)}, u32[]{:S(2)}) copy-start(s32[512]{0:T(512)} %param.31) | copy-start | bytes 6148
  10.0 149.7 %collective-permute-start.1 = (bf16[1,32,256]{2,1,0:T(8,128)(2,1)S(1)}, bf16[1,32,256]{2,1,0:T(8,128)(2,1)S(1)}, u32[]{:S(2)}, u32[]{:S(2)}) collective-permute-start(bf16[1,32,256]{2,1,0:T(8,128)(2,1)S(1)} %get-tuple-element.51), channel_id=1, source_target_pairs={{16,0},{32,16},{48,32},{64,48},{80,64},{96,80},{112,96},{128,112},... | collective-permute-start | bytes 49160 | tf_op jit(solution)/shard_map/ppermute | solution.py:19
  11.9 107.2 %collective-permute-start = (bf16[1,32,256]{2,1,0:T(8,128)(2,1)S(1)}, bf16[1,32,256]{2,1,0:T(8,128)(2,1)S(1)}, u32[]{:S(2)}, u32[]{:S(2)}) collective-permute-start(bf16[1,32,256]{2,1,0:T(8,128)(2,1)S(1)} %get-tuple-element.52), channel_id=1, source_target_pairs={{0,16},{16,32},{32,48},{48,64},{64,80},{80,96},{96,112},{112,128},... | collective-permute-start | bytes 49160 | tf_op jit(solution)/shard_map/ppermute | solution.py:19
  197.2 1.3 copy-start.4
  197.2 1.3 copy-start.11
  201.5 122.9 %collective-permute-start.3 = (bf16[1,32,256]{2,1,0:T(8,128)(2,1)S(1)}, bf16[1,32,256]{2,1,0:T(8,128)(2,1)S(1)}, u32[]{:S(2)}, u32[]{:S(2)}) collective-permute-start(bf16[1,32,256]{2,1,0:T(8,128)(2,1)S(1)} %get-tuple-element.45), channel_id=1, source_target_pairs={{16,0},{32,16},{48,32},{64,48},{80,64},{96,80},{112,96},{128,112},... | collective-permute-start | bytes 49160 | tf_op jit(solution)/shard_map/ppermute | solution.py:19
  203.5 80.7 %collective-permute-start.2 = (bf16[1,32,256]{2,1,0:T(8,128)(2,1)S(1)}, bf16[1,32,256]{2,1,0:T(8,128)(2,1)S(1)}, u32[]{:S(2)}, u32[]{:S(2)}) collective-permute-start(bf16[1,32,256]{2,1,0:T(8,128)(2,1)S(1)} %get-tuple-element.46), channel_id=1, source_target_pairs={{0,16},{16,32},{32,48},{48,64},{64,80},{80,96},{96,112},{112,128},... | collective-permute-start | bytes 49160 | tf_op jit(solution)/shard_map/ppermute | solution.py:19
  362.9 1.3 copy-start.5
  362.9 1.3 copy-start.12
  367.6 0.8 copy-start.7
  367.6 0.8 copy-start.8
  487.0 2.5 copy-start.3
  492.3 1.2 copy-start.6
  494.6 0.8 copy-start.2
  495.4 0.9 copy-start.1
Sparse Core Ops, SparseCore 0:
  369.6 97.2 all-gather.1
where the time goes:
time: 504 us; the launch traced here: 503 us
  blocking collectives  316 us (63%)
  waiting for transfers between devices  82.8 us (16%)
  between operations  35.8 us (7%)
  local copies, waits for them, and re-layouts  32 us (6%)
  other arithmetic  16.2 us (3%)
  matrix products  11.8 us (2%)
  starting transfers between devices  8.66 us (2%)
    all_gather x2, blocking collectives, fetch_halo(): lax.all_gather(shortened(part[:, -width:]), 'lon', axis=0, tiled=True)  83.2 us
    all_gather x1, waiting for transfers between devices, on_device(): piece = lax.all_gather(key_val, 'lon', axis=1, tiled=True)  82.8 us
    all_gather x2, blocking collectives, fetch_halo(): lax.all_gather(shortened(from_north), 'lon', axis=0, tiled=True)  80.8 us
    all_gather x2, blocking collectives, fetch_halo(): lax.all_gather(shortened(part[:, :width]), 'lon', axis=0, tiled=True)  77.4 us
    all_gather x2, blocking collectives, fetch_halo(): lax.all_gather(shortened(from_south), 'lon', axis=0, tiled=True)  74.5 us
    unnamed x28, local copies, waits for them, and re-layouts  13.4 us
  transfers between devices with their start and end apart: 5, of which 1 were waited for; matrix products, arithmetic and copies ran while one was open for 3% of the time, Pallas kernels for 0%

commit v1 on v0

--- a/solution.py
+++ b/solution.py
@@ -145,7 +145,8 @@
     root_dim = math.sqrt(head_dim)
     heads_q = query.reshape(block_size, block_size, heads, head_dim)
     row_limits = lax.dynamic_slice_in_dim(counts, first_row, block_size)
-    piece = lax.all_gather(key_val, "lon", axis=1, tiled=True)
+    sent = jnp.stack([key_val] * lax.axis_size("lon"))
+    piece = jnp.concatenate(lax.all_to_all(sent, "lon", 0, 0), axis=1)
     summed = jnp.zeros((block_size, block_size, heads, head_dim), jnp.float32)
     peak = jnp.full((block_size, block_size, heads), -jnp.inf, jnp.float32)
     total = jnp.zeros((block_size, block_size, heads), jnp.float32)

time: 504 us -> 459 us (0.911)
  waiting for transfers between devices: 82.8 us -> 43.6 us
  between operations: 35.8 us -> 21.9 us
  local copies, waits for them, and re-layouts: 32 us -> 18.7 us
  starting transfers between devices: 8.66 us -> 19.5 us
  blocking collectives: 316 us -> 324 us
    all_gather x1 -> x0, waiting for transfers between devices: 82.8 us -> none  [on_device(): piece = lax.all_gather(key_val, 'lon', axis=1, tiled=True)]
    all_to_all x0 -> x1, waiting for transfers between devices: none -> 43.6 us  [on_device(): piece = jnp.concatenate(lax.all_to_all(sent, 'lon', 0, 0), axis=1)]
    all_to_all x0 -> x1, starting transfers between devices: none -> 10.8 us  [on_device(): piece = jnp.concatenate(lax.all_to_all(sent, 'lon', 0, 0), axis=1)]
    unnamed x28 -> x24, local copies, waits for them, and re-layouts: 13.4 us -> 3.53 us
    all_gather x2, blocking collectives: 74.5 us -> 82.6 us  [fetch_halo(): lax.all_gather(shortened(from_south), 'lon', axis=0, tiled=True)]
    slice x1 -> x0, local copies, waits for them, and re-layouts: 7.59 us -> none  [on_device(): piece[:, :, :head_dim]]
where the time goes in v1:
time: 459 us; the launch traced here: 456 us
  blocking collectives  324 us (71%)
  waiting for transfers between devices  43.6 us (9%)
  between operations  21.9 us (5%)
  starting transfers between devices  19.5 us (4%)
  local copies, waits for them, and re-layouts  18.7 us (4%)
  other arithmetic  16 us (3%)
  matrix products  12.4 us (3%)
    all_gather x2, blocking collectives, fetch_halo(): lax.all_gather(shortened(part[:, -width:]), 'lon', axis=0, tiled=True)  83.2 us
    all_gather x2, blocking collectives, fetch_halo(): lax.all_gather(shortened(from_south), 'lon', axis=0, tiled=True)  82.6 us
    all_gather x2, blocking collectives, fetch_halo(): lax.all_gather(shortened(from_north), 'lon', axis=0, tiled=True)  80.8 us
    all_gather x2, blocking collectives, fetch_halo(): lax.all_gather(shortened(part[:, :width]), 'lon', axis=0, tiled=True)  77.4 us
    all_to_all x1, waiting for transfers between devices, on_device(): piece = jnp.concatenate(lax.all_to_all(sent, 'lon', 0, 0), axis=1)  43.6 us
    all_to_all x1, starting transfers between devices, on_device(): piece = jnp.concatenate(lax.all_to_all(sent, 'lon', 0, 0), axis=1)  10.8 us
  transfers between devices with their start and end apart: 5, of which 1 were waited for; matrix products, arithmetic and copies ran while one was open for 3% of the time, Pallas kernels for 0%

profile of v1, /device:TPU:2, one launch (start us, length us, event | category | flops | bytes accessed | tf_op | source)
XLA Modules:
  0.0 456.2 jit_solution(6393467648494600784)
XLA Ops:
  0.0 1.3 dynamic_slice.73
  2.0 1.1 conditional.2
  2.0 1.1 rev.22
  3.4 1.9 collective-permute-start.1
  5.4 2.4 collective-permute-start
  7.8 0.6 dynamic_slice.74
  11.5 0.3 select_reduce_fusion
  12.5 0.7 fusion.78
  16.1 46.0 %all_gather.25 = bf16[512,1,256]{2,0,1:T(8,128)(2,1)S(1)} all-gather(bf16[32,1,256]{2,0,1:T(8,128)(2,1)S(1)} %get-tuple-element.53), channel_id=1, replica_groups=mesh['lat'=16,'lon'=16] {'lon'}, dimensions={0}, use_global_device_ids=true | all-gather | bytes 278528 | tf_op jit(solution)/shard_map/all_gather | solution.py:53
  62.7 36.9 %all_gather.26 = bf16[512,1,256]{2,0,1:T(8,128)(2,1)S(1)} all-gather(bf16[32,1,256]{2,0,1:T(8,128)(2,1)S(1)} %get-tuple-element.54), channel_id=1, replica_groups=mesh['lat'=16,'lon'=16] {'lon'}, dimensions={0}, use_global_device_ids=true | all-gather | bytes 278528 | tf_op jit(solution)/shard_map/all_gather | solution.py:52
  100.4 0.4 pad_maximum_fusion.2
  112.0 40.5 %all_gather.24 = bf16[16,32,256]{2,1,0:T(8,128)(2,1)S(1)} all-gather(bf16[1,32,256]{2,1,0:T(8,128)(2,1)S(1)} %collective-permute-done), channel_id=1, replica_groups=mesh['lat'=16,'lon'=16] {'lon'}, dimensions={0}, use_global_device_ids=true | all-gather | bytes 278528 | tf_op jit(solution)/shard_map/all_gather | solution.py:54
  152.6 37.0 %all_gather.27 = bf16[16,32,256]{2,1,0:T(8,128)(2,1)S(1)} all-gather(bf16[1,32,256]{2,1,0:T(8,128)(2,1)S(1)} %collective-permute-done.1), channel_id=1, replica_groups=mesh['lat'=16,'lon'=16] {'lon'}, dimensions={0}, use_global_device_ids=true | all-gather | bytes 278528 | tf_op jit(solution)/shard_map/all_gather | solution.py:55
  189.6 0.5 maximum_maximum_fusion.1
  190.1 0.8 fusion.72
  190.9 0.4 copy-done.3
  194.5 1.9 collective-permute-start.3
  196.4 2.4 collective-permute-start.2
  198.8 40.5 %all_gather.30 = bf16[512,1,256]{2,0,1:T(8,128)(2,1)S(1)} all-gather(bf16[32,1,256]{2,0,1:T(8,128)(2,1)S(1)} %copy.116), channel_id=1, replica_groups=mesh['lat'=16,'lon'=16] {'lon'}, dimensions={0}, use_global_device_ids=true | all-gather | bytes 278528 | tf_op jit(solution)/shard_map/all_gather | solution.py:52
  239.4 37.2 %all_gather.29 = bf16[512,1,256]{2,0,1:T(8,128)(2,1)S(1)} all-gather(bf16[32,1,256]{2,0,1:T(8,128)(2,1)S(1)} %copy.115), channel_id=1, replica_groups=mesh['lat'=16,'lon'=16] {'lon'}, dimensions={0}, use_global_device_ids=true | all-gather | bytes 278528 | tf_op jit(solution)/shard_map/all_gather | solution.py:53
  276.7 0.4 pad_maximum_fusion
  277.1 40.2 %all_gather.28 = bf16[16,32,256]{2,1,0:T(8,128)(2,1)S(1)} all-gather(bf16[1,32,256]{2,1,0:T(8,128)(2,1)S(1)} %collective-permute-done.2), channel_id=1, replica_groups=mesh['lat'=16,'lon'=16] {'lon'}, dimensions={0}, use_global_device_ids=true | all-gather | bytes 278528 | tf_op jit(solution)/shard_map/all_gather | solution.py:54
  317.4 45.6 %all_gather.31 = bf16[16,32,256]{2,1,0:T(8,128)(2,1)S(1)} all-gather(bf16[1,32,256]{2,1,0:T(8,128)(2,1)S(1)} %collective-permute-done.3), channel_id=1, replica_groups=mesh['lat'=16,'lon'=16] {'lon'}, dimensions={0}, use_global_device_ids=true | all-gather | bytes 278528 | tf_op jit(solution)/shard_map/all_gather | solution.py:55
  363.0 0.5 maximum_maximum_fusion.3
  363.5 0.4 fusion.70
  363.9 0.4 fusion.71
  364.3 0.9 copy-done.4
  366.3 0.5 convolution_add_fusion.4
  368.0 0.5 multiply_reduce_fusion
  368.9 0.4 copy-done.6
  369.6 2.8 stack.3
  372.4 10.8 %all-to-all-start = ((bf16[16,32,32,128]{3,2,1,0:T(8,128)(2,1)}), bf16[16,32,32,128]{3,2,1,0:T(8,128)(2,1)}, u32[]{:S(2)}, u32[]{:S(2)}) async-start(bf16[16,32,32,128]{3,2,1,0:T(8,128)(2,1)} %stack.3), calls=%async_computation | async-start | bytes 8388608 | tf_op jit(solution)/shard_map/all_to_all | solution.py:149
  385.4 0.7 fusion.80
  386.1 4.5 compare_select_fusion.1
  390.6 5.4 %fusion.59 = s32[512]{0:T(512)S(1)} fusion(pred[512]{0:T(512)(128)(4,1)S(1)} %get-tuple-element.93, pred[512]{0:T(512)(128)(4,1)S(1)} %get-tuple-element.94, pred[512]{0:T(512)(128)(4,1)S(1)} %get-tuple-element.95, pred[512]{0:T(512)(128)(4,1)S(1)} %get-tuple-element.96, pred[512]{0:T(512)(128)(4,1)S(1)} %get-tuple-element.97, ...), kind=kLoop, calls=%fused_computation.145 | loop fusion | flops 8704 | bytes 8740 | tf_op jit(solution)/shard_map/add | solution.py:154
  396.4 0.4 reshape_reshape.3
  396.8 43.6 %all-to-all-done = bf16[16,32,32,128]{3,2,1,0:T(8,128)(2,1)} async-done(((bf16[16,32,32,128]{3,2,1,0:T(8,128)(2,1)}), bf16[16,32,32,128]{3,2,1,0:T(8,128)(2,1)}, u32[]{:S(2)}, u32[]{:S(2)}) %all-to-all-start) | async-done | bytes 4194336 | tf_op jit(solution)/shard_map/all_to_all | solution.py:149
  440.4 3.3 copy.121
  443.7 1.6 fusion
  445.4 2.4 fusion.1
  447.8 4.4 divide_convert_fusion
  452.2 0.5 copy.125
  452.8 0.7 dot_general.93
  453.4 0.3 fusion.13
  453.8 0.7 conditional.3
  453.8 0.4 rev.23
  454.5 0.8 copy-done.2
  455.3 0.9 copy-done.1
  (86 shorter events, 7.8 us)
Async XLA Ops:
  0.0 396.1 %copy-start = (bf16[256,256]{1,0:T(8,128)(2,1)S(1)}, bf16[256,256]{1,0:T(8,128)(2,1)}, u32[]{:S(2)}) copy-start(bf16[256,256]{1,0:T(8,128)(2,1)} %param.25) | copy-start | bytes 393220
  2.0 5.8 %copy-start.8 = (s32[16,16]{1,0:T(8,128)S(1)}, s32[16,16]{1,0:T(8,128)}, u32[]{:S(2)}) copy-start(s32[16,16]{1,0:T(8,128)} %param.30) | copy-start | bytes 3076
  2.0 13.7 %copy-start.9 = (s32[512]{0:T(512)S(1)}, s32[512]{0:T(512)}, u32[]{:S(2)}) copy-start(s32[512]{0:T(512)} %param.31) | copy-start | bytes 6148
  3.4 149.1 %collective-permute-start.1 = (bf16[1,32,256]{2,1,0:T(8,128)(2,1)S(1)}, bf16[1,32,256]{2,1,0:T(8,128)(2,1)S(1)}, u32[]{:S(2)}, u32[]{:S(2)}) collective-permute-start(bf16[1,32,256]{2,1,0:T(8,128)(2,1)S(1)} %get-tuple-element.49), channel_id=1, source_target_pairs={{16,0},{32,16},{48,32},{64,48},{80,64},{96,80},{112,96},{128,112},... | collective-permute-start | bytes 49160 | tf_op jit(solution)/shard_map/ppermute | solution.py:19
  5.4 106.7 %collective-permute-start = (bf16[1,32,256]{2,1,0:T(8,128)(2,1)S(1)}, bf16[1,32,256]{2,1,0:T(8,128)(2,1)S(1)}, u32[]{:S(2)}, u32[]{:S(2)}) collective-permute-start(bf16[1,32,256]{2,1,0:T(8,128)(2,1)S(1)} %get-tuple-element.50), channel_id=1, source_target_pairs={{0,16},{16,32},{32,48},{48,64},{64,80},{80,96},{96,112},{112,128},... | collective-permute-start | bytes 49160 | tf_op jit(solution)/shard_map/ppermute | solution.py:19
  190.1 1.3 copy-start.3
  190.1 1.3 copy-start.10
  194.5 122.9 %collective-permute-start.3 = (bf16[1,32,256]{2,1,0:T(8,128)(2,1)S(1)}, bf16[1,32,256]{2,1,0:T(8,128)(2,1)S(1)}, u32[]{:S(2)}, u32[]{:S(2)}) collective-permute-start(bf16[1,32,256]{2,1,0:T(8,128)(2,1)S(1)} %get-tuple-element.43), channel_id=1, source_target_pairs={{16,0},{32,16},{48,32},{64,48},{80,64},{96,80},{112,96},{128,112},... | collective-permute-start | bytes 49160 | tf_op jit(solution)/shard_map/ppermute | solution.py:19
  196.4 80.7 %collective-permute-start.2 = (bf16[1,32,256]{2,1,0:T(8,128)(2,1)S(1)}, bf16[1,32,256]{2,1,0:T(8,128)(2,1)S(1)}, u32[]{:S(2)}, u32[]{:S(2)}) collective-permute-start(bf16[1,32,256]{2,1,0:T(8,128)(2,1)S(1)} %get-tuple-element.44), channel_id=1, source_target_pairs={{0,16},{16,32},{32,48},{48,64},{64,80},{80,96},{96,112},{112,128},... | collective-permute-start | bytes 49160 | tf_op jit(solution)/shard_map/ppermute | solution.py:19
  363.9 1.3 copy-start.4
  363.9 1.3 copy-start.11
  368.6 0.8 copy-start.6
  368.6 0.8 copy-start.7
  372.4 68.0 %all-to-all-start = ((bf16[16,32,32,128]{3,2,1,0:T(8,128)(2,1)}), bf16[16,32,32,128]{3,2,1,0:T(8,128)(2,1)}, u32[]{:S(2)}, u32[]{:S(2)}) async-start(bf16[16,32,32,128]{3,2,1,0:T(8,128)(2,1)} %stack.3), calls=%async_computation | async-start | bytes 8388608 | tf_op jit(solution)/shard_map/all_to_all | solution.py:149
  452.2 1.2 copy-start.5
  454.5 0.8 copy-start.2
  455.3 0.9 copy-start.1
